TPU v7x, 256 devices: a whole 4x4x8 slice. The times are simulated.
256 devices in a mesh: dp: 4 (over x), expert: 64 (over y, z, core).
Axes of the slice: x: 4, y: 4, z: 8, core: 2. Of those that a mesh axis runs over, the one named last changes fastest.
Arguments:
- tokens: bfloat16 [8192, 2048], P('expert'), may hold values from -4 to 4
- norm_gain: bfloat16 [2048], replicated, may hold values from 0.5 to 1.5
- routing_projection_matrix: bfloat16 [2048, 64], replicated, may hold values from -0.125 to 0.125
- experts: int32 [8192, 8], P('expert'), may hold values from 0 to 63, as said below
- replica_key: int32 [8192, 8], P('expert'), may hold values from 0 to 1048575
- slot_expert: int32 [128], replicated, may hold values from 0 to 63, as said below
- capacity: int32 [128], replicated, may hold values from 4 to 16, as said below
- slot_gate_up_weight: bfloat16 [128, 2048, 2, 1024], P('expert', None, None, 'dp'), may hold values from -0.125 to 0.125
- down_weight: bfloat16 [128, 1024, 2048], P('expert', 'dp'), may hold values from -0.1875 to 0.1875
Outputs:
- mixed: bfloat16 [8192, 2048], P('expert', 'dp')
Inputs may be any that keep to these rules, and one draw needn't show every extreme that they name: Each row names 8 different experts. `slot_expert`: every expert occupies at least one slot. `capacity`: for every j the capacities of slots 2 * j and 2 * j + 1 sum to at most 24, and to exactly 24 for some j.
All inputs are finite; a program needn't handle non-finite values.
Results may differ from a plain program's by a relative error of at most 0.012.
Values may be sent and summed in bfloat16 or wider, within the bound.
A program may use at most 128 MiB of HBM per device.

v0:
```python
import jax
import jax.numpy as jnp
from jax import lax
from jax.sharding import PartitionSpec as P

CAPACITY_HIGH = 16
CAP_DEV = 24


def assign_slots(experts, replica_key, slot_expert):
    flat_experts = experts.reshape(-1)
    holders = (flat_experts[:, None] == slot_expert[None, :]).astype(jnp.int32)
    copies = jnp.sum(holders, axis=1)
    earlier = jnp.cumsum(holders, axis=1) - holders
    wanted = replica_key.reshape(-1) % copies
    matched = holders * (earlier == wanted[:, None]).astype(jnp.int32)
    numbers = jnp.arange(slot_expert.shape[0], dtype=jnp.int32)
    return jnp.sum(matched * numbers[None, :], axis=1)


def slot_partial(flat_rows, gate_up_one, down_one):
    model_width = flat_rows.shape[1]
    unit_count = gate_up_one.shape[2]
    gate_up_out = jnp.dot(
        flat_rows,
        gate_up_one.reshape(model_width, 2 * unit_count),
        preferred_element_type=jnp.float32,
    )
    activated = (jax.nn.silu(gate_up_out[:, :unit_count]) * gate_up_out[:, unit_count:]).astype(
        jnp.bfloat16
    )
    result = jnp.dot(activated, down_one, preferred_element_type=jnp.float32)
    return result.astype(jnp.bfloat16)


def on_device(
    tokens,
    norm_gain,
    routing_projection_matrix,
    experts,
    replica_key,
    slot_expert,
    capacity,
    slot_gate_up_weight,
    down_weight,
):
    peer_count = lax.axis_size("expert")
    group_count = lax.axis_size("dp")
    group_pos = lax.axis_index("dp")
    me = lax.axis_index("expert")
    rows_here = tokens.shape[0]
    model_width = tokens.shape[1]
    pick_count = experts.shape[1]
    slot_count = slot_expert.shape[0]
    per_device = slot_count // peer_count
    quarter = model_width // group_count
    buffer_rows = CAP_DEV
    hidden = tokens.astype(jnp.float32)
    scale = lax.rsqrt(jnp.mean(hidden * hidden, axis=-1, keepdims=True) + 1e-06)
    normed = (hidden * scale * norm_gain.astype(jnp.float32)).astype(jnp.bfloat16)
    logits = jnp.dot(normed, routing_projection_matrix, preferred_element_type=jnp.float32)
    score = jax.nn.sigmoid(jnp.take_along_axis(logits, experts, axis=1)).reshape(-1)
    slot_ids = assign_slots(experts, replica_key, slot_expert)
    onehot = (slot_ids[:, None] == jnp.arange(slot_count, dtype=jnp.int32)[None, :]).astype(
        jnp.int32
    )
    position = jnp.sum((jnp.cumsum(onehot, axis=0) - onehot) * onehot, axis=1)
    slot_cap = jnp.sum(onehot * capacity[None, :], axis=1)
    kept_mask = position < slot_cap
    is_second = slot_ids % per_device == 1
    row_in = jnp.where(is_second, buffer_rows - slot_cap + position, position)
    target = jnp.where(
        kept_mask, slot_ids // per_device * buffer_rows + row_in, peer_count * buffer_rows
    )
    source_rows = jnp.arange(rows_here * pick_count, dtype=jnp.int32) // pick_count
    normed_part = lax.dynamic_slice_in_dim(normed, group_pos * quarter, quarter, 1)
    outgoing = (
        jnp.zeros((peer_count * buffer_rows + 1, quarter), jnp.bfloat16)
        .at[target]
        .set(normed_part[source_rows])
    )
    outgoing = outgoing[:-1].reshape(peer_count, buffer_rows, quarter)
    incoming_part = lax.all_to_all(outgoing, "expert", split_axis=0, concat_axis=0, tiled=True)
    incoming = lax.all_gather(incoming_part, "dp", axis=2, tiled=True)
    flat_in = incoming.reshape(peer_count * buffer_rows, model_width)
    first_out = slot_partial(flat_in, slot_gate_up_weight[0], down_weight[0])
    second_out = slot_partial(flat_in, slot_gate_up_weight[1], down_weight[1])
    first_cap = lax.dynamic_index_in_dim(capacity, me * per_device, keepdims=False)
    row_index = jnp.arange(peer_count * buffer_rows, dtype=jnp.int32) % buffer_rows
    partial_value = jnp.where((row_index < first_cap)[:, None], first_out, second_out)
    partial_value = partial_value.reshape(peer_count, buffer_rows, model_width)
    summed = lax.psum_scatter(partial_value, "dp", scatter_dimension=2, tiled=True)
    returned = lax.all_to_all(summed, "expert", split_axis=0, concat_axis=0, tiled=True)
    flat_ret = returned.reshape(peer_count * buffer_rows, quarter)
    flat_ret = jnp.concatenate([flat_ret, jnp.zeros((1, quarter), flat_ret.dtype)])
    weight_kept = jnp.where(kept_mask, score, jnp.float32(0.0))
    gathered = flat_ret[target].astype(jnp.float32).reshape(rows_here, pick_count, quarter)
    mixture = jnp.sum(weight_kept.reshape(rows_here, pick_count)[:, :, None] * gathered, axis=1)
    residual = lax.dynamic_slice_in_dim(tokens, group_pos * quarter, quarter, 1).astype(jnp.float32)
    return (residual + mixture).astype(jnp.bfloat16)


def solution(mesh):
    in_specs = (
        P("expert", None),
        P(),
        P(),
        P("expert", None),
        P("expert", None),
        P(),
        P(),
        P("expert", None, None, "dp"),
        P("expert", "dp", None),
    )
    out_specs = P("expert", "dp")
    return jax.shard_map(
        on_device, mesh=mesh, in_specs=in_specs, out_specs=out_specs, check_vma=False
    )
```

profile of v0, /device:TPU:1, one launch (start us, length us, event | category | flops | bytes accessed | tf_op | source)
XLA Modules:
  0.0 289.3 jit_solution(4413022350040989855)
XLA Ops:
  6.6 0.8 copy.21
  7.5 0.8 convert_reduce_fusion
  8.3 0.8 compare_convert_fusion
  9.0 1.2 fusion.3
  10.3 0.7 convert_element_type.50
  11.0 0.8 copy.22
  11.9 0.5 reduce_window_sum.26
  12.5 0.2 fusion.19
  12.8 0.2 fusion.23
  13.1 0.3 copy.24
  13.9 0.5 copy-done.2
  14.4 10.1 %scatter_custom_fusion = bf16[1537,512]{1,0:T(8,128)(2,1)S(1)} fusion(s32[1024]{0:T(1024)S(1)} %bitcast.69, bf16[128,512]{1,0:T(8,128)(2,1)S(1)} %constant_dynamic-slice_fusion, s32[1024]{0:T(1024)S(1)} %broadcast_clamp_fusion.1, bf16[]{:T(256)} %constant.114.clone.1), kind=kCustom, calls=%fused_computation.20 | custom fusion | bytes 1573890 | tf_op jit(solution)/shard_map/scatter | solution.py:80
  24.6 52.9 %all_to_all.10 = bf16[64,24,512]{2,1,0:T(8,128)(2,1)} all-to-all(bf16[64,24,512]{2,1,0:T(8,128)(2,1)S(1)} %bitcast.59), channel_id=1, replica_groups=mesh['dp'=4,'expert'=64] {'expert'}, dimensions={0} | all-to-all | bytes 3145728 | tf_op jit(solution)/shard_map/all_to_all | solution.py:83
  77.5 0.2 reduce-scatter.2.cloned.1.call-start
  77.7 0.6 dynamic_slice.11
  78.3 4.7 %fusion.32 = (bf16[1,2048,2,256]{3,2,1,0:T(2,128)(2,1)S(1)}, bf16[1,2048,2,256]{3,2,1,0:T(2,128)(2,1)S(1)}) fusion(bf16[2,2048,2,256]{3,2,1,0:T(2,128)(2,1)} %param.16), kind=kLoop, calls=%fused_computation.77 | loop fusion | bytes 8388608 | tf_op jit(solution)/shard_map/slice | solution.py:86
  83.0 0.5 copy.30
  83.5 1.8 copy.31
  85.4 0.7 fusion.26
  86.0 56.6 %all-gather.2.cloned.1.call-done = bf16[64,24,2048]{2,1,0:T(8,128)(2,1)} async-done(((bf16[64,24,512]{2,1,0:T(8,128)(2,1)}), bf16[64,24,2048]{2,1,0:T(8,128)(2,1)}) %all-gather.2.cloned.1.call-update) | async-done | bytes 6291472 | tf_op jit(solution)/shard_map/all_gather | solution.py:84
  142.6 6.3 %fusion.35 = f32[1536,512]{1,0:T(8,128)S(1)} fusion(bf16[1536,2048]{1,0:T(8,128)(2,1)} %bitcast.71, bf16[2048,512]{1,0:T(8,128)(2,1)} %bitcast.62), kind=kOutput, calls=%fused_computation.80 | convolution fusion | flops 3221225472 | bytes 11534336 | tf_op jit(solution)/shard_map/dot_general | solution.py:24
  148.9 3.5 %fusion.34 = f32[1536,512]{1,0:T(8,128)S(1)} fusion(bf16[1536,2048]{1,0:T(8,128)(2,1)S(1)} %bitcast.72, bf16[2048,512]{1,0:T(8,128)(2,1)S(1)} %bitcast.61), kind=kOutput, calls=%fused_computation.79 | convolution fusion | flops 3221225472 | bytes 11534336 | tf_op jit(solution)/shard_map/dot_general | solution.py:24
  152.4 1.9 convolution_convert_fusion
  154.3 3.9 %broadcast_select_fusion = bf16[1536,2048]{1,0:T(8,128)(2,1)} fusion(bf16[1536,2048]{1,0:T(8,128)(2,1)S(1)} %convolution_convert_fusion, pred[1536]{0:T(1024)(128)(4,1)S(1)} %fusion.26, bf16[2,256,2048]{2,1,0:T(8,128)(2,1)S(1)} %copy-done.8, f32[1536,512]{1,0:T(8,128)S(1)} %fusion.34), kind=kOutput, calls=%fused_computation.6 | convolution fusion | flops 1619263488 | bytes 16779264 | tf_op jit(solution)/shard_map/dot_general | solution.py:32
  158.3 67.4 %reduce-scatter.2.cloned.1.call-done = bf16[64,24,512]{2,1,0:T(8,128)(2,1)} async-done(((bf16[64,24,2048]{2,1,0:T(8,128)(2,1)}), bf16[64,24,512]{2,1,0:T(8,128)(2,1)}) %reduce-scatter.2.cloned.1.call-update) | async-done | bytes 1572880 | tf_op jit(solution)/shard_map/reduce_scatter | solution.py:92
  225.7 10.6 %all-to-all-start.1 = ((bf16[64,24,512]{2,1,0:T(8,128)(2,1)}), bf16[64,24,512]{2,1,0:T(8,128)(2,1)S(1)}, u32[]{:S(2)}, u32[]{:S(2)}) async-start(bf16[64,24,512]{2,1,0:T(8,128)(2,1)} %reduce-scatter.2.cloned.1.call-done), calls=%async_computation.2 | async-start | bytes 3145728 | tf_op jit(solution)/shard_map/all_to_all | solution.py:93
  236.6 0.3 fusion.33
  236.9 7.0 %gather_fusion.1 = f32[1024]{0:T(1024)S(1)} fusion(f32[128,64]{0,1:T(8,128)S(1)} %fusion.33, s32[1024]{0:T(1024)S(1)} %reshape.274), kind=kCustom, calls=%fused_computation.2 | custom fusion | bytes 16384 | tf_op jit(solution)/shard_map/jit(take_along_axis)/gather | solution.py:62
  244.4 31.7 %all-to-all-done.1 = bf16[64,24,512]{2,1,0:T(8,128)(2,1)S(1)} async-done(((bf16[64,24,512]{2,1,0:T(8,128)(2,1)}), bf16[64,24,512]{2,1,0:T(8,128)(2,1)S(1)}, u32[]{:S(2)}, u32[]{:S(2)}) %all-to-all-start.1) | async-done | bytes 1572896 | tf_op jit(solution)/shard_map/all_to_all | solution.py:93
  276.2 4.0 %gather_fusion = bf16[1024,512]{1,0:T(8,128)(2,1)S(1)} fusion(bf16[1537,512]{1,0:T(8,128)(2,1)S(1)} %concatenate.3, s32[1024]{0:T(1024)S(1)} %broadcast_clamp_fusion), kind=kCustom, calls=%fused_computation.1 | custom fusion | bytes 2101248 | tf_op jit(solution)/shard_map/gather | solution.py:97
  280.2 0.7 fusion
  280.9 1.6 add_convert_fusion
  (48 shorter events, 1.9 us)
Async XLA Ops:
  6.5 230.0 %copy-start = (bf16[2048,64]{0,1:T(8,128)(2,1)S(1)}, bf16[2048,64]{0,1:T(8,128)(2,1)}, u32[]{:S(2)}) copy-start(bf16[2048,64]{0,1:T(8,128)(2,1)} %param.11) | copy-start | bytes 786436
  6.5 5.9 %copy-start.5 = (s32[128]{0:T(128)S(1)}, s32[128]{0:T(128)}, u32[]{:S(2)}) copy-start(s32[128]{0:T(128)} %param.14) | copy-start | bytes 1540
  6.5 136.1 %all-gather.2.cloned.1.call-start = ((), (), s32[]{:S(2)}) async-start(), calls=%async_computation.3 | async-start | bytes 7864320 | tf_op jit(solution)/shard_map/all_gather | solution.py:84
  11.9 1.5 copy-start.1
  12.7 0.9 copy-start.6
  13.6 0.8 copy-start.2
  77.5 148.1 %reduce-scatter.2.cloned.1.call-start = ((), (), s32[]{:S(2)}) async-start(), calls=%async_computation.4 | async-start | bytes 7864320 | tf_op jit(solution)/shard_map/reduce_scatter | solution.py:92
  142.6 6.3 %copy-start.7 = (bf16[64,24,2048]{2,1,0:T(8,128)(2,1)S(1)}, bf16[64,24,2048]{2,1,0:T(8,128)(2,1)}, u32[]{:S(2)}) copy-start(bf16[64,24,2048]{2,1,0:T(8,128)(2,1)} %all-gather.2.cloned.1.call-done) | copy-start | bytes 18874372
  148.9 3.5 %copy-start.8 = (bf16[2,256,2048]{2,1,0:T(8,128)(2,1)S(1)}, bf16[2,256,2048]{2,1,0:T(8,128)(2,1)}, u32[]{:S(2)}) copy-start(bf16[2,256,2048]{2,1,0:T(8,128)(2,1)} %param.17) | copy-start | bytes 6291460
  158.2 78.1 %copy-start.4 = (s32[128,8]{0,1:T(8,128)S(1)}, s32[128,8]{0,1:T(8,128)}, u32[]{:S(2)}) copy-start(s32[128,8]{0,1:T(8,128)} %param.12) | copy-start | bytes 12292
  158.3 78.3 %copy-start.3 = (bf16[128,2048]{1,0:T(8,128)(2,1)S(1)}, bf16[128,2048]{1,0:T(8,128)(2,1)}, u32[]{:S(2)}) copy-start(bf16[128,2048]{1,0:T(8,128)(2,1)} %copy-done.2) | copy-start | bytes 1572868
  225.7 50.4 %all-to-all-start.1 = ((bf16[64,24,512]{2,1,0:T(8,128)(2,1)}), bf16[64,24,512]{2,1,0:T(8,128)(2,1)S(1)}, u32[]{:S(2)}, u32[]{:S(2)}) async-start(bf16[64,24,512]{2,1,0:T(8,128)(2,1)} %reduce-scatter.2.cloned.1.call-done), calls=%async_computation.2 | async-start | bytes 3145728 | tf_op jit(solution)/shard_map/all_to_all | solution.py:93
Sparse Core Ops, SparseCore 0:
  77.6 64.9 all-gather.1
  158.4 67.2 reduce-scatter.1
where the time goes:
time: 290 us; the launch traced here: 289 us
  waiting for transfers between devices  156 us (54%)
  blocking collectives  52.9 us (18%)
  local copies, waits for them, and re-layouts  32.3 us (11%)
  matrix products  15.8 us (5%)
  between operations  13.8 us (5%)
  starting transfers between devices  10.9 us (4%)
  other arithmetic  7.97 us (3%)
    reduce_scatter x1, waiting for transfers between devices, on_device(): lax.psum_scatter(partial_value, 'dp', scatter_dimension=2, tiled=True)  67.4 us
    all_gather x1, waiting for transfers between devices, on_device(): incoming = lax.all_gather(incoming_part, 'dp', axis=2, tiled=True)  56.6 us
    all_to_all x1, blocking collectives, on_device(): lax.all_to_all(outgoing, 'expert', split_axis=0, concat_axis=0, tiled=True)  52.9 us
    all_to_all x1, waiting for transfers between devices, on_device(): lax.all_to_all(summed, 'expert', split_axis=0, concat_axis=0, tiled=True)  31.7 us
    all_to_all x1, starting transfers between devices, on_device(): lax.all_to_all(summed, 'expert', split_axis=0, concat_axis=0, tiled=True)  10.6 us
    scatter x1, local copies, waits for them, and re-layouts, on_device(): outgoing = jnp.zeros((peer_count * buffer_rows + 1, quarter), jnp.bfloat1...  10.1 us
    dot_general x2, matrix products, slot_partial(): jnp.dot(flat_rows, gate_up_one.reshape(model_width, 2 * unit_count), pref...  9.76 us
    gather x5, local copies, waits for them, and re-layouts, on_device(): jnp.take_along_axis(logits, experts, axis=1)  7.34 us
  transfers between devices with their start and end apart: 3, of which 3 were waited for; matrix products, arithmetic and copies ran while one was open for 6% of the time, Pallas kernels for 0%

commit v1 on v0

--- a/solution.py
+++ b/solution.py
@@ -81,7 +81,9 @@
     )
     outgoing = outgoing[:-1].reshape(peer_count, buffer_rows, quarter)
     incoming_part = lax.all_to_all(outgoing, "expert", split_axis=0, concat_axis=0, tiled=True)
-    incoming = lax.all_gather(incoming_part, "dp", axis=2, tiled=True)
+    incoming = jnp.concatenate(
+        lax.all_to_all(jnp.stack([incoming_part] * lax.axis_size("dp")), "dp", 0, 0), axis=2
+    )
     flat_in = incoming.reshape(peer_count * buffer_rows, model_width)
     first_out = slot_partial(flat_in, slot_gate_up_weight[0], down_weight[0])
     second_out = slot_partial(flat_in, slot_gate_up_weight[1], down_weight[1])

time: 290 us -> 310 us (1.069)
  local copies, waits for them, and re-layouts: 32.3 us -> 50.8 us
  starting transfers between devices: 10.9 us -> 15.9 us
    all_to_all x0 -> x1, waiting for transfers between devices: none -> 61.4 us  [on_device(): lax.all_to_all(jnp.stack([incoming_part] * lax.axis_size('dp')), 'dp', 0, 0)]
    all_gather x1 -> x0, waiting for transfers between devices: 56.6 us -> none  [on_device(): incoming = lax.all_gather(incoming_part, 'dp', axis=2, tiled=True)]
    reshape x0 -> x1, local copies, waits for them, and re-layouts: none -> 10.9 us  [on_device(): jnp.concatenate(lax.all_to_all(jnp.stack([incoming_part] * lax.axis_size(...]
    reduce_scatter x1, waiting for transfers between devices: 67.4 us -> 61.9 us  [on_device(): lax.psum_scatter(partial_value, 'dp', scatter_dimension=2, tiled=True)]
    all_to_all x0 -> x1, starting transfers between devices: none -> 5.24 us  [on_device(): lax.all_to_all(jnp.stack([incoming_part] * lax.axis_size('dp')), 'dp', 0, 0)]
    unnamed x22 -> x25, local copies, waits for them, and re-layouts: 4.48 us -> 8.83 us
    another operation x3 -> x4, local copies, waits for them, and re-layouts: 0.28 us -> 3.45 us  [the longest x1 3.17 us: on_device(): jnp.stack([incoming_part] * lax.axis_size('dp'))]
where the time goes in v1:
time: 310 us; the launch traced here: 309 us
  waiting for transfers between devices  155 us (50%)
  blocking collectives  52.7 us (17%)
  local copies, waits for them, and re-layouts  50.8 us (16%)
  starting transfers between devices  15.9 us (5%)
  between operations  13.8 us (4%)
  matrix products  13.1 us (4%)
  other arithmetic  7.97 us (3%)
    reduce_scatter x1, waiting for transfers between devices, on_device(): lax.psum_scatter(partial_value, 'dp', scatter_dimension=2, tiled=True)  61.9 us
    all_to_all x1, waiting for transfers between devices, on_device(): lax.all_to_all(jnp.stack([incoming_part] * lax.axis_size('dp')), 'dp', 0, 0)  61.4 us
    all_to_all x1, blocking collectives, on_device(): lax.all_to_all(outgoing, 'expert', split_axis=0, concat_axis=0, tiled=True)  52.7 us
    all_to_all x1, waiting for transfers between devices, on_device(): lax.all_to_all(summed, 'expert', split_axis=0, concat_axis=0, tiled=True)  31.7 us
    reshape x1, local copies, waits for them, and re-layouts, on_device(): jnp.concatenate(lax.all_to_all(jnp.stack([incoming_part] * lax.axis_size(...  10.9 us
    all_to_all x1, starting transfers between devices, on_device(): lax.all_to_all(summed, 'expert', split_axis=0, concat_axis=0, tiled=True)  10.6 us
    scatter x1, local copies, waits for them, and re-layouts, on_device(): outgoing = jnp.zeros((peer_count * buffer_rows + 1, quarter), jnp.bfloat1...  10.1 us
    unnamed x25, local copies, waits for them, and re-layouts  8.83 us
  transfers between devices with their start and end apart: 3, of which 3 were waited for; matrix products, arithmetic and copies ran while one was open for 6% of the time, Pallas kernels for 0%

profile of v1, /device:TPU:1, one launch (start us, length us, event | category | flops | bytes accessed | tf_op | source)
XLA Modules:
  0.0 309.5 jit_solution(16890288595434931676)
XLA Ops:
  6.6 0.8 copy.31
  7.5 0.8 convert_reduce_fusion
  8.3 0.8 compare_convert_fusion
  9.0 1.2 fusion.3
  10.3 0.7 convert_element_type.50
  11.0 0.8 copy.32
  11.9 0.5 reduce_window_sum.26
  13.9 0.5 copy-done.2
  14.4 10.1 %scatter_custom_fusion = bf16[1537,512]{1,0:T(8,128)(2,1)S(1)} fusion(s32[1024]{0:T(1024)S(1)} %bitcast.75, bf16[128,512]{1,0:T(8,128)(2,1)S(1)} %constant_dynamic-slice_fusion, s32[1024]{0:T(1024)S(1)} %broadcast_clamp_fusion.1, bf16[]{:T(256)} %constant.114.clone.1), kind=kCustom, calls=%fused_computation.20 | custom fusion | bytes 1573890 | tf_op jit(solution)/shard_map/scatter | solution.py:80
  24.6 52.7 %all_to_all.15 = bf16[64,24,512]{2,1,0:T(8,128)(2,1)S(1)} all-to-all(bf16[64,24,512]{2,1,0:T(8,128)(2,1)S(1)} %bitcast.65), channel_id=1, replica_groups=mesh['dp'=4,'expert'=64] {'expert'}, dimensions={0} | all-to-all | bytes 3145728 | tf_op jit(solution)/shard_map/all_to_all | solution.py:83
  77.4 3.2 %stack.2 = bf16[4,64,24,512]{3,2,1,0:T(8,128)(2,1)} broadcast(bf16[64,24,512]{2,1,0:T(8,128)(2,1)S(1)} %all_to_all.15), dimensions={1,2,3} | broadcast | bytes 7864320 | tf_op jit(solution)/shard_map/stack | solution.py:85
  80.6 5.2 %all-to-all-start.1 = ((bf16[4,64,24,512]{3,2,1,0:T(8,128)(2,1)}), bf16[4,64,24,512]{3,2,1,0:T(8,128)(2,1)}, u32[]{:S(2)}, u32[]{:S(2)}) async-start(bf16[4,64,24,512]{3,2,1,0:T(8,128)(2,1)} %stack.2), calls=%async_computation.1 | async-start | bytes 12582912 | tf_op jit(solution)/shard_map/all_to_all | solution.py:85
  85.9 0.6 dynamic_slice.11
  86.4 4.9 %fusion.32 = (bf16[1,2048,2,256]{3,2,1,0:T(2,128)(2,1)S(1)}, bf16[1,2048,2,256]{3,2,1,0:T(2,128)(2,1)S(1)}) fusion(bf16[2,2048,2,256]{3,2,1,0:T(2,128)(2,1)} %param.16), kind=kLoop, calls=%fused_computation.77 | loop fusion | bytes 8388608 | tf_op jit(solution)/shard_map/slice | solution.py:88
  91.3 1.9 copy.42
  93.2 1.9 copy.43
  95.0 0.7 fusion.26
  95.7 61.4 %all-to-all-done.1 = bf16[4,64,24,512]{3,2,1,0:T(8,128)(2,1)} async-done(((bf16[4,64,24,512]{3,2,1,0:T(8,128)(2,1)}), bf16[4,64,24,512]{3,2,1,0:T(8,128)(2,1)}, u32[]{:S(2)}, u32[]{:S(2)}) %all-to-all-start.1) | async-done | bytes 6291488 | tf_op jit(solution)/shard_map/all_to_all | solution.py:85
  157.1 10.9 %copy.39 = bf16[64,24,4,512]{3,2,1,0:T(4,128)(2,1)S(1)} copy(bf16[64,24,4,512]{3,1,0,2:T(8,128)(2,1)} %bitcast.11) | data formatting | bytes 12582912 | tf_op jit(solution)/shard_map/reshape | solution.py:84
  168.0 2.9 copy.41
  171.0 3.4 %fusion.35 = f32[1536,512]{1,0:T(8,128)S(1)} fusion(bf16[1536,2048]{1,0:T(8,128)(2,1)S(1)} %bitcast.63, bf16[2048,512]{1,0:T(8,128)(2,1)S(1)} %bitcast.68), kind=kOutput, calls=%fused_computation.80 | convolution fusion | flops 3221225472 | bytes 11534336 | tf_op jit(solution)/shard_map/dot_general | solution.py:24
  174.4 3.5 %fusion.34 = f32[1536,512]{1,0:T(8,128)S(1)} fusion(bf16[1536,2048]{1,0:T(8,128)(2,1)S(1)} %bitcast.64, bf16[2048,512]{1,0:T(8,128)(2,1)S(1)} %bitcast.67), kind=kOutput, calls=%fused_computation.79 | convolution fusion | flops 3221225472 | bytes 11534336 | tf_op jit(solution)/shard_map/dot_general | solution.py:24
  177.9 1.9 convolution_convert_fusion
  179.8 4.1 %broadcast_select_fusion = bf16[1536,2048]{1,0:T(8,128)(2,1)} fusion(bf16[1536,2048]{1,0:T(8,128)(2,1)S(1)} %convolution_convert_fusion, pred[1536]{0:T(1024)(128)(4,1)S(1)} %fusion.26, bf16[2,256,2048]{2,1,0:T(8,128)(2,1)S(1)} %copy-done.9, f32[1536,512]{1,0:T(8,128)S(1)} %fusion.34), kind=kOutput, calls=%fused_computation.6 | convolution fusion | flops 1619263488 | bytes 16779264 | tf_op jit(solution)/shard_map/dot_general | solution.py:32
  183.9 61.9 %reduce-scatter.2.cloned.1.call-done = bf16[64,24,512]{2,1,0:T(8,128)(2,1)} async-done(((bf16[64,24,2048]{2,1,0:T(8,128)(2,1)}), bf16[64,24,512]{2,1,0:T(8,128)(2,1)}) %reduce-scatter.2.cloned.1.call-update) | async-done | bytes 1572880 | tf_op jit(solution)/shard_map/reduce_scatter | solution.py:94
  245.8 10.6 %all-to-all-start.2 = ((bf16[64,24,512]{2,1,0:T(8,128)(2,1)}), bf16[64,24,512]{2,1,0:T(8,128)(2,1)S(1)}, u32[]{:S(2)}, u32[]{:S(2)}) async-start(bf16[64,24,512]{2,1,0:T(8,128)(2,1)} %reduce-scatter.2.cloned.1.call-done), calls=%async_computation.3 | async-start | bytes 3145728 | tf_op jit(solution)/shard_map/all_to_all | solution.py:95
  256.7 0.3 fusion.33
  257.0 7.0 %gather_fusion.1 = f32[1024]{0:T(1024)S(1)} fusion(f32[128,64]{0,1:T(8,128)S(1)} %fusion.33, s32[1024]{0:T(1024)S(1)} %reshape.276), kind=kCustom, calls=%fused_computation.2 | custom fusion | bytes 16384 | tf_op jit(solution)/shard_map/jit(take_along_axis)/gather | solution.py:62
  264.5 31.7 %all-to-all-done.2 = bf16[64,24,512]{2,1,0:T(8,128)(2,1)S(1)} async-done(((bf16[64,24,512]{2,1,0:T(8,128)(2,1)}), bf16[64,24,512]{2,1,0:T(8,128)(2,1)S(1)}, u32[]{:S(2)}, u32[]{:S(2)}) %all-to-all-start.2) | async-done | bytes 1572896 | tf_op jit(solution)/shard_map/all_to_all | solution.py:95
  296.3 4.0 %gather_fusion = bf16[1024,512]{1,0:T(8,128)(2,1)S(1)} fusion(bf16[1537,512]{1,0:T(8,128)(2,1)S(1)} %concatenate.3, s32[1024]{0:T(1024)S(1)} %broadcast_clamp_fusion), kind=kCustom, calls=%fused_computation.1 | custom fusion | bytes 2101248 | tf_op jit(solution)/shard_map/gather | solution.py:99
  300.3 0.7 fusion
  301.0 1.6 add_convert_fusion
  (52 shorter events, 2.6 us)
Async XLA Ops:
  6.5 250.1 %copy-start = (bf16[2048,64]{0,1:T(8,128)(2,1)S(1)}, bf16[2048,64]{0,1:T(8,128)(2,1)}, u32[]{:S(2)}) copy-start(bf16[2048,64]{0,1:T(8,128)(2,1)} %param.11) | copy-start | bytes 786436
  6.5 5.9 %copy-start.7 = (s32[128]{0:T(128)S(1)}, s32[128]{0:T(128)}, u32[]{:S(2)}) copy-start(s32[128]{0:T(128)} %param.14) | copy-start | bytes 1540
  11.9 1.5 copy-start.1
  12.7 0.9 copy-start.8
  13.6 0.8 copy-start.2
  80.6 76.6 %all-to-all-start.1 = ((bf16[4,64,24,512]{3,2,1,0:T(8,128)(2,1)}), bf16[4,64,24,512]{3,2,1,0:T(8,128)(2,1)}, u32[]{:S(2)}, u32[]{:S(2)}) async-start(bf16[4,64,24,512]{3,2,1,0:T(8,128)(2,1)} %stack.2), calls=%async_computation.1 | async-start | bytes 12582912 | tf_op jit(solution)/shard_map/all_to_all | solution.py:85
  85.8 160.0 %reduce-scatter.2.cloned.1.call-start = ((), (), s32[]{:S(2)}) async-start(), calls=%async_computation.4 | async-start | bytes 7864320 | tf_op jit(solution)/shard_map/reduce_scatter | solution.py:94
  168.0 3.0 copy-start.5
  171.0 3.5 %copy-start.4 = (bf16[256,8,2,256]{3,1,2,0:T(8,128)(2,1)S(1)}, bf16[256,8,2,256]{3,1,2,0:T(8,128)(2,1)}, u32[]{:S(2)}) copy-start(bf16[256,8,2,256]{3,1,2,0:T(8,128)(2,1)} %copy.42) | copy-start | bytes 6291460
  174.4 3.5 %copy-start.9 = (bf16[2,256,2048]{2,1,0:T(8,128)(2,1)S(1)}, bf16[2,256,2048]{2,1,0:T(8,128)(2,1)}, u32[]{:S(2)}) copy-start(bf16[2,256,2048]{2,1,0:T(8,128)(2,1)} %param.17) | copy-start | bytes 6291460
  183.9 72.6 %copy-start.6 = (s32[128,8]{0,1:T(8,128)S(1)}, s32[128,8]{0,1:T(8,128)}, u32[]{:S(2)}) copy-start(s32[128,8]{0,1:T(8,128)} %param.12) | copy-start | bytes 12292
  183.9 72.8 %copy-start.3 = (bf16[128,2048]{1,0:T(8,128)(2,1)S(1)}, bf16[128,2048]{1,0:T(8,128)(2,1)}, u32[]{:S(2)}) copy-start(bf16[128,2048]{1,0:T(8,128)(2,1)} %copy-done.2) | copy-start | bytes 1572868
  245.8 50.4 %all-to-all-start.2 = ((bf16[64,24,512]{2,1,0:T(8,128)(2,1)}), bf16[64,24,512]{2,1,0:T(8,128)(2,1)S(1)}, u32[]{:S(2)}, u32[]{:S(2)}) async-start(bf16[64,24,512]{2,1,0:T(8,128)(2,1)} %reduce-scatter.2.cloned.1.call-done), calls=%async_computation.3 | async-start | bytes 3145728 | tf_op jit(solution)/shard_map/all_to_all | solution.py:95
Sparse Core Ops, SparseCore 0:
  184.0 61.7 reduce-scatter.1
